TPU v7x, 32 devices: a whole 2x2x4 slice. The times are simulated.
32 devices in a mesh: parts: 2 (over x), rows: 16 (over z, y, core).
Axes of the slice: x: 2, y: 2, z: 4, core: 2. Of those that a mesh axis runs over, the one named last changes fastest.
Arguments:
- estimate: float32 [256, 2048], P(('parts', 'rows')), parts along dimension 0, may hold values from -6 to 6
- observed: float32 [256, 2048], P('parts', 'rows'), parts along dimension 0, may hold values from -6 to 6
- cotangent: float32 [256, 2048], P(('parts', 'rows')), parts along dimension 0
- zone_map: int32 [2, 16], P('parts'), parts along dimension 0, may hold values from 0 to 7
- bank_pick: int32 [2, 8], replicated, may hold values from 0 to 7
- psf_bank: float32 [8, 25], replicated, may hold values from 0.01 to 1
- w_first: bfloat16 [32, 1, 3, 3], replicated, may hold values from -2 to 2
- w_mid: bfloat16 [32, 32, 3, 3], replicated, may hold values from -0.375 to 0.375
- w_last: bfloat16 [1, 32, 3, 3], replicated, may hold values from -0.375 to 0.375
Outputs:
- denoised: float32 [256, 2048], P(('parts', 'rows')), parts along dimension 0
- grad_estimate: float32 [256, 2048], P(('parts', 'rows')), parts along dimension 0
- grad_first: float32 [64, 1, 3, 3], P('parts'), parts along dimension 0
- grad_mid: float32 [64, 32, 3, 3], P('parts'), parts along dimension 0
- grad_last: float32 [2, 32, 3, 3], P('parts'), parts along dimension 0
There are 2 independent parts, one for each index of `parts`. A program takes and returns all parts, laid end to end along the dimension named above; an argument that names none is the same for every part. Nothing has to cross between parts.
All inputs are finite; a program needn't handle non-finite values.
Results may differ from a plain program's by a relative error of at most 0.0071.
Values may be sent and summed in bfloat16 or wider, within the bound.
A program may use at most 256 MiB of HBM per device.

v0:
```python
import math
import jax
import jax.numpy as jnp
from jax import lax
from jax.sharding import PartitionSpec as P

BLK = 128
RAD = 12
STEP_SIZE = 2.0
GRAD_FACTOR = 8.0


def padded_2(shard, sides, width):
    for axis, dim in sides:
        size, length = (lax.axis_size(axis), shard.shape[dim])
        up = [(i, (i + 1) % size) for i in range(size - 1)]
        down = [(j, i) for i, j in up]
        last = lax.slice_in_dim(shard, length - width, length, axis=dim)
        leading = lax.slice_in_dim(shard, 0, width, axis=dim)
        before = lax.ppermute(last, axis, up)
        after = lax.ppermute(leading, axis, down)
        shard = jnp.concatenate([before, shard, after], axis=dim)
    return shard


def silu_slope(values):
    sigmoid = jax.nn.sigmoid(values)
    return sigmoid * (1.0 + values * (1.0 - sigmoid))


def flipped(weight):
    return jnp.transpose(jnp.flip(weight, (2, 3)), (1, 0, 2, 3))


def conv_rim(padded, weight):
    padding = ((0, 0), (1, 1))
    result = lax.conv_general_dilated(
        padded[None],
        weight,
        (1, 1),
        padding,
        dimension_numbers=("NCHW", "OIHW", "NCHW"),
        preferred_element_type=jnp.float32,
    )
    return result[0]


def weight_taps(framed, errors):
    height_cells = errors.shape[1]
    width_cells = errors.shape[2]
    all_taps = []
    for tap_row in range(3):
        line_taps = []
        for tap_col in range(3):
            window = framed[:, tap_row : tap_row + height_cells, tap_col : tap_col + width_cells]
            line_taps.append(
                jnp.einsum("ohw,chw->oc", errors, window, preferred_element_type=jnp.float32)
            )
        all_taps.append(jnp.stack(line_taps, axis=-1))
    return jnp.stack(all_taps, axis=-2)


def weight_grad(padded, errors, rim_dim):
    widths = [(0, 0), (0, 0), (0, 0)]
    widths[3 - rim_dim] = (1, 1)
    framed = jnp.pad(padded, widths)
    return weight_taps(framed, errors)


def blur_line(values, tap_coef, along, adjoint):
    length = values.shape[along]
    widths = [(0, 0), (0, 0)]
    widths[along] = (RAD, RAD)
    summed = jnp.zeros_like(values)
    padded = jnp.pad(values, widths)
    for offset in range(2 * RAD + 1):
        factor = tap_coef[offset][None, :] if along == 1 else tap_coef[offset][:, None]
        if adjoint:
            spread = jnp.pad(factor * values, widths)
            summed = summed + lax.slice_in_dim(
                spread, 2 * RAD - offset, 2 * RAD - offset + length, axis=along
            )
        else:
            summed = summed + factor * lax.slice_in_dim(padded, offset, offset + length, axis=along)
    return summed


def zone_kernels(psf_bank, bank_pick):
    norm_bank = psf_bank / jnp.sum(psf_bank, axis=1, keepdims=True)
    select = (
        bank_pick[:, :, None] == jnp.arange(psf_bank.shape[0], dtype=jnp.int32)[None, None, :]
    ).astype(jnp.float32)
    return jnp.einsum("rzb,bt->rzt", select, norm_bank, precision=lax.Precision.HIGHEST)


def tap_table(zone_line, kernel_table):
    zone_count = kernel_table.shape[0]
    onehot = (zone_line[:, None] == jnp.arange(zone_count, dtype=jnp.int32)[None, :]).astype(
        jnp.float32
    )
    per_block = jnp.einsum("nz,zt->tn", onehot, kernel_table, precision=lax.Precision.HIGHEST)
    tap_count = per_block.shape[0]
    block_count = per_block.shape[1]
    return jnp.broadcast_to(per_block[:, :, None], (tap_count, block_count, BLK)).reshape(
        tap_count, block_count * BLK
    )


def data_gradient(values, target, row_coef, col_coef):
    blurred = blur_line(values, row_coef, 1, False)
    columns = lax.all_to_all(blurred, "rows", split_axis=1, concat_axis=0, tiled=True)
    columns = blur_line(columns, col_coef, 0, False)
    if target is not None:
        columns = columns - target
    spread = blur_line(columns, col_coef, 0, True)
    back_rows = lax.all_to_all(spread, "rows", split_axis=0, concat_axis=1, tiled=True)
    return blur_line(back_rows, row_coef, 1, True)


def band_rims(values):
    return padded_2(values, (("rows", 1),), 1)


def denoise(data_step, cotangent, w_first, w_mid, w_last, add_rims, rim_dim):
    first_in = data_step.astype(jnp.bfloat16)[None]
    first_pad = add_rims(first_in)
    pre_first = conv_rim(first_pad, w_first)
    act_first = jax.nn.silu(pre_first).astype(jnp.bfloat16)
    first_act_pad = add_rims(act_first)
    pre_mid = conv_rim(first_act_pad, w_mid)
    act_mid = jax.nn.silu(pre_mid).astype(jnp.bfloat16)
    mid_act_pad = add_rims(act_mid)
    denoised = data_step + conv_rim(mid_act_pad, w_last)[0]
    cot_in = cotangent.astype(jnp.bfloat16)[None]
    cot_pad = add_rims(cot_in)
    back_mid = (conv_rim(cot_pad, flipped(w_last)) * silu_slope(pre_mid)).astype(jnp.bfloat16)
    back_mid_pad = add_rims(back_mid)
    back_first = (conv_rim(back_mid_pad, flipped(w_mid)) * silu_slope(pre_first)).astype(
        jnp.bfloat16
    )
    back_first_pad = add_rims(back_first)
    grad_data = cotangent + conv_rim(back_first_pad, flipped(w_first))[0]
    grad_last = weight_grad(mid_act_pad, cot_in, rim_dim)
    grad_mid = weight_grad(first_act_pad, back_mid, rim_dim)
    grad_first = weight_grad(first_pad, back_first, rim_dim)
    return (denoised, grad_data, (grad_first, grad_mid, grad_last))


def on_device(estimate, observed, cotangent, zone_map, bank_pick, psf_bank, w_first, w_mid, w_last):
    band_rows = estimate.shape[0]
    width = estimate.shape[1]
    group_cols = observed.shape[1]
    position = lax.axis_index("rows")
    height = band_rows * lax.axis_size("rows")
    kernels = zone_kernels(psf_bank, bank_pick)
    col_line = lax.dynamic_slice_in_dim(zone_map, position * group_cols // BLK, 1, 1)[:, 0]
    col_coef = tap_table(col_line, kernels[1])
    row_line = lax.dynamic_slice_in_dim(zone_map, position * band_rows // BLK, 1, 0)[0]
    row_coef = tap_table(row_line, kernels[0])
    data_step = estimate - STEP_SIZE * data_gradient(estimate, observed, row_coef, col_coef)
    denoised, grad_data, partial_grads = denoise(
        data_step, cotangent, w_first, w_mid, w_last, band_rims, 1
    )
    grad_estimate = grad_data - STEP_SIZE * data_gradient(grad_data, None, row_coef, col_coef)
    grad_scale = GRAD_FACTOR / math.sqrt(height * width)
    grad_first, grad_mid, grad_last = lax.psum(
        (
            partial_grads[0] * grad_scale,
            partial_grads[1] * grad_scale,
            partial_grads[2] * grad_scale,
        ),
        "rows",
    )
    return (denoised, grad_estimate, grad_first, grad_mid, grad_last)


def solution(mesh):
    placed = (
        P(("parts", "rows"), None),
        P("parts", "rows"),
        P(("parts", "rows"), None),
        P("parts", None),
        P(),
        P(),
        P(),
        P(),
        P(),
    )
    return jax.shard_map(
        on_device,
        mesh=mesh,
        in_specs=placed,
        out_specs=(
            P(("parts", "rows"), None),
            P(("parts", "rows"), None),
            P("parts", None, None, None),
            P("parts", None, None, None),
            P("parts", None, None, None),
        ),
        check_vma=False,
    )
```

profile of v0, /device:TPU:0, one launch (start us, length us, event | category | flops | bytes accessed | tf_op | source)
XLA Modules:
  0.0 456.3 jit_solution(8213222737690068692)
XLA Ops:
  13.1 9.3 %all-to-all-start = ((f32[8,16,128]{2,0,1:T(8,128)}), f32[8,16,128]{2,0,1:T(8,128)S(1)}, u32[]{:S(2)}, u32[]{:S(2)}) async-start(f32[8,16,128]{2,0,1:T(8,128)} %add_bitcast_fusion.1), calls=%async_computation | async-start | bytes 131072 | tf_op jit(solution)/shard_map/all_to_all | solution.py:111
  29.3 16.7 %broadcast_multiply_fusion.47 = (f32[128,128]{1,0:T(8,128)S(1)}, f32[128,128]{1,0:T(8,128)S(1)}) fusion(f32[]{:T(128)} %bitcast.9, f32[128,128]{1,0:T(8,128)} %param.10, f32[]{:T(128)} %bitcast.61, f32[]{:T(128)} %bitcast.60, f32[]{:T(128)} %bitcast.59, f32[]{:T(128)} %bitcast.58, f32[]{:T(128)} %bitcast.57, f32[]{:T(128)} %bitcast.56, f32[]{:T(128)} %bitcast.55, ...), kind=kLoop, calls=%fused_computation.672 | loop fusion | flops 835584 | bytes 262244 | tf_op jit(solution)/shard_map/mul | solution.py:79
  49.4 11.4 %broadcast_multiply_fusion.45 = (f32[128,128]{1,0:T(8,128)S(1)}, f32[128,128]{1,0:T(8,128)S(1)}, f32[128,128]{1,0:T(8,128)S(1)}, f32[128,128]{1,0:T(8,128)S(1)},...) fusion(f32[128,128]{1,0:T(8,128)S(1)} %get-tuple-element.38, ...), kind=kLoop, calls=%fused_computation.670 | loop fusion | flops 294912 | bytes 1245256 | tf_op jit(solution)/shard_map/mul | solution.py:79
  67.9 5.3 %all-to-all-done.1 = f32[16,8,128]{2,1,0:T(8,128)S(1)} async-done(((f32[16,8,128]{2,1,0:T(8,128)}), f32[16,8,128]{2,1,0:T(8,128)S(1)}, u32[]{:S(2)}, u32[]{:S(2)}) %all-to-all-start.1) | async-done | bytes 65568 | tf_op jit(solution)/shard_map/all_to_all | solution.py:116
  78.0 7.6 %fusion.358 = f32[8,8,257,32]{3,1,2,0:T(8,128)} fusion(bf16[1,10,8,259]{2,0,3,1:T(2,128)(2,1)S(1)} %copy.104, bf16[32,1,3,3]{0,3,2,1:T(4,128)(2,1)S(1)} %bitcast.471), kind=kOutput, calls=%fused_computation.709 | convolution fusion | flops 9474048 | bytes 2147360 | tf_op jit(solution)/shard_map/conv_general_dilated | solution.py:37
  85.6 7.2 %copy.106 = f32[8,8,257,32]{2,3,1,0:T(8,128)} copy(f32[8,8,257,32]{3,1,2,0:T(8,128)} %fusion.358) | data formatting | bytes 4210688 | tf_op jit(solution)/shard_map/conv_general_dilated | solution.py:37
  95.1 7.6 %fusion.361 = f32[8,8,257,32]{3,1,2,0:T(8,128)} fusion(bf16[1,10,8,259]{2,0,3,1:T(2,128)(2,1)S(1)} %copy.92, bf16[32,1,3,3]{0,3,2,1:T(4,128)(2,1)S(1)} %copy-done.80), kind=kOutput, calls=%fused_computation.712 | convolution fusion | flops 9474048 | bytes 2147360 | tf_op jit(solution)/shard_map/conv_general_dilated | solution.py:37
  102.7 5.9 %copy.94 = f32[8,8,257,32]{2,3,1,0:T(8,128)S(1)} copy(f32[8,8,257,32]{3,1,2,0:T(8,128)} %fusion.361) | data formatting | bytes 4210688 | tf_op jit(solution)/shard_map/conv_general_dilated | solution.py:37
  126.9 4.9 %reshape.468 = bf16[32,10,1,8,257]{4,3,0,1,2:T(8,128)(2,1)} reshape(bf16[32,10,1,2056]{3,0,1,2:T(8,128)(2,1)} %pad.422) | data formatting | bytes 2631680 | tf_op jit(solution)/shard_map/conv_general_dilated | solution.py:37
  131.8 7.5 %copy.97 = bf16[32,10,1,8,257]{0,3,4,1,2:T(8,128)(2,1)} copy(bf16[32,10,1,8,257]{4,3,0,1,2:T(8,128)(2,1)} %reshape.468) | data formatting | bytes 2631680 | tf_op jit(solution)/shard_map/conv_general_dilated | solution.py:37
  140.2 11.1 %fusion.6 = f32[8,8,257,32]{3,1,2,0:T(8,128)} fusion(bf16[32,32,3,3]{1,0,3,2:T(8,128)(2,1)S(1)} %copy-done, bf16[32,10,1,7,2]{0,3,4,1,2:T(8,128)(2,1)S(1)} %slice.1495, bf16[32,10,1,8,257]{0,3,4,1,2:T(8,128)(2,1)} %copy.97), kind=kOutput, calls=%fused_computation.7 | convolution fusion | flops 307147776 | bytes 3448576 | tf_op jit(solution)/shard_map/conv_general_dilated | solution.py:37
  151.2 7.1 %copy.98 = f32[8,8,257,32]{2,3,1,0:T(8,128)} copy(f32[8,8,257,32]{3,1,2,0:T(8,128)} %fusion.6) | data formatting | bytes 4210688 | tf_op jit(solution)/shard_map/conv_general_dilated | solution.py:37
  158.3 6.4 %multiply_convert_fusion.1 = (bf16[8,8,257,32]{2,3,1,0:T(8,128)(2,1)}, f32[8,8,257,32]{2,3,1,0:T(8,128)S(1)}, f32[8,8,257,32]{2,3,1,0:T(8,128)}) fusion(f32[8,8,257,32]{2,3,1,0:T(8,128)} %copy.98, pred[8,257]{1,0:T(8,128)(4,1)S(1)} %copy-done.79, f32[8,8,257,32]{2,3,1,0:T(8,128)} %copy.106), kind=kLoop, calls=%fused_computation.32 | loop fusion | flops 5789696 | bytes 9476104 | tf_op jit(solution)/shard_map/convert_element_type | solution.py:136
  172.3 5.3 %copy.99 = f32[8,8,257,32]{2,1,3,0:T(8,128)} copy(f32[8,8,257,32]{2,3,1,0:T(8,128)} %get-tuple-element.41) | data formatting | bytes 4210688 | tf_op jit(solution)/shard_map/conv_general_dilated | solution.py:37
  177.6 4.4 reshape.472
  196.1 6.1 %collective-permute-start.4 = (bf16[32,1,2048]{2,0,1:T(8,128)(2,1)}, bf16[32,1,2048]{2,0,1:T(8,128)(2,1)}, u32[]{:S(2)}, u32[]{:S(2)}) collective-permute-start(bf16[32,1,2048]{2,0,1:T(8,128)(2,1)} %get-tuple-element.55), channel_id=1, source_target_pairs={{0,1},{1,2},{2,3},{3,4},{4,5},{5,6},{6,7},{7,8},{8,9},{9,10},{10,1... | collective-permute-start | bytes 393224 | tf_op jit(solution)/shard_map/ppermute | solution.py:20
  221.4 7.5 %copy.101 = bf16[32,10,1,8,257]{0,3,4,1,2:T(8,128)(2,1)} copy(bf16[32,10,1,8,257]{4,3,0,1,2:T(8,128)(2,1)} %reshape.475) | data formatting | bytes 2631680 | tf_op jit(solution)/shard_map/conv_general_dilated | solution.py:37
  229.8 11.8 %broadcast_select_fusion.1 = f32[8,8,257,1]{3,1,2,0:T(8,128)} fusion(pred[8,257]{0,1:T(8,128)(4,1)S(1)} %copy-done.82, bf16[32,10,1,7,2]{0,3,4,1,2:T(8,128)(2,1)S(1)} %slice.1499, bf16[32,10,1,8,257]{0,3,4,1,2:T(8,128)(2,1)} %copy.101, bf16[1,32,3,3]{1,3,2,0:T(4,128)(2,1)S(1)} %copy-done.81), kind=kOutput, calls=%fused_computation.30 | convolution fusion | flops 13468736 | bytes 1393224 | tf_op jit(solution)/shard_map/conv_general_dilated | solution.py:37
  241.5 6.1 %copy.103 = f32[8,8,257,1]{2,1,0,3:T(8,128)S(1)} copy(f32[8,8,257,1]{3,1,2,0:T(8,128)} %broadcast_select_fusion.1) | data formatting | bytes 131584 | tf_op jit(solution)/shard_map/conv_general_dilated | solution.py:37
  248.4 5.3 %copy.109 = bf16[32,10,1,8,257]{0,3,4,1,2:T(8,128)(2,1)} copy(bf16[32,10,1,8,257]{4,3,0,1,2:T(8,128)(2,1)S(1)} %reshape.491) | data formatting | bytes 2631680 | tf_op jit(solution)/shard_map/conv_general_dilated | solution.py:37
  254.5 11.2 %fusion.14 = f32[8,8,257,32]{3,1,2,0:T(8,128)} fusion(bf16[32,32,3,3]{1,0,3,2:T(8,128)(2,1)S(1)} %copy-done, bf16[32,10,1,7,2]{0,3,4,1,2:T(8,128)(2,1)S(1)} %slice.1507, bf16[32,10,1,8,257]{0,3,4,1,2:T(8,128)(2,1)} %copy.109), kind=kOutput, calls=%fused_computation.13 | convolution fusion | flops 307147776 | bytes 3448576 | tf_op jit(solution)/shard_map/conv_general_dilated | solution.py:37
  265.7 7.3 %copy.110 = f32[8,8,257,32]{2,3,1,0:T(8,128)} copy(f32[8,8,257,32]{3,1,2,0:T(8,128)} %fusion.14) | data formatting | bytes 4210688 | tf_op jit(solution)/shard_map/conv_general_dilated | solution.py:37
  273.0 5.6 %multiply_convert_fusion.2 = (bf16[8,8,257,32]{2,3,1,0:T(8,128)(2,1)S(1)}, bf16[8,8,257,32]{2,3,1,0:T(8,128)(2,1)}, f32[8,8,257,32]{2,3,1,0:T(8,128)}) fusion(f32[8,8,257,32]{2,3,1,0:T(8,128)S(1)} %copy-done.2, pred[8,257]{1,0:T(8,128)(4,1)S(1)} %copy-done.79, f32[8,8,257,32]{2,3,1,0:T(8,128)} %copy.110), kind=kLoop, calls=%fused_computation.33 | loop fusion | flops 6842368 | bytes 8423432 | tf_op jit(solution)/shard_map/convert_element_type | solution.py:128
  290.9 4.3 reshape.495
  297.8 5.5 %collective-permute-start.10 = (bf16[32,1,2048]{2,0,1:T(8,128)(2,1)S(1)}, bf16[32,1,2048]{2,0,1:T(8,128)(2,1)S(1)}, u32[]{:S(2)}, u32[]{:S(2)}) collective-permute-start(bf16[32,1,2048]{2,0,1:T(8,128)(2,1)S(1)} %get-tuple-element.51), channel_id=1, source_target_pairs={{0,1},{1,2},{2,3},{3,4},{4,5},{5,6},{6,7},{7,8},{8,9},{9,10},{10,1... | collective-permute-start | bytes 393224 | tf_op jit(solution)/shard_map/ppermute | solution.py:20
  309.9 5.2 %copy.113 = bf16[32,10,1,8,257]{0,3,4,1,2:T(8,128)(2,1)} copy(bf16[32,10,1,8,257]{4,3,0,1,2:T(8,128)(2,1)S(1)} %reshape.500) | data formatting | bytes 2631680 | tf_op jit(solution)/shard_map/conv_general_dilated | solution.py:37
  315.8 11.8 %broadcast_select_fusion = f32[8,8,257,1]{3,1,2,0:T(8,128)} fusion(pred[8,257]{0,1:T(8,128)(4,1)S(1)} %copy-done.83, bf16[32,10,1,7,2]{0,3,4,1,2:T(8,128)(2,1)S(1)} %slice.1511, bf16[32,10,1,8,257]{0,3,4,1,2:T(8,128)(2,1)} %copy.113, bf16[1,32,3,3]{1,3,2,0:T(4,128)(2,1)S(1)} %bitcast.470), kind=kOutput, calls=%fused_computation.29 | convolution fusion | flops 13468736 | bytes 1393224 | tf_op jit(solution)/shard_map/conv_general_dilated | solution.py:37
  327.6 6.3 %copy.115 = f32[8,8,257,1]{2,1,0,3:T(8,128)S(1)} copy(f32[8,8,257,1]{3,1,2,0:T(8,128)} %broadcast_select_fusion) | data formatting | bytes 131584 | tf_op jit(solution)/shard_map/conv_general_dilated | solution.py:37
  339.3 8.8 %all-to-all-start.2 = ((f32[8,16,128]{2,0,1:T(8,128)}), f32[8,16,128]{2,0,1:T(8,128)S(1)}, u32[]{:S(2)}, u32[]{:S(2)}) async-start(f32[8,16,128]{2,0,1:T(8,128)} %add_bitcast_fusion), calls=%async_computation.2 | async-start | bytes 131072 | tf_op jit(solution)/shard_map/all_to_all | solution.py:111
  355.1 15.9 %broadcast_multiply_fusion.46 = (f32[128,128]{1,0:T(8,128)S(1)}, f32[128,128]{1,0:T(8,128)S(1)}) fusion(f32[]{:T(128)} %bitcast.9, f32[]{:T(128)} %bitcast.61, f32[]{:T(128)} %bitcast.60, f32[]{:T(128)} %bitcast.59, f32[]{:T(128)} %bitcast.58, f32[]{:T(128)} %bitcast.57, f32[]{:T(128)} %bitcast.56, f32[]{:T(128)} %bitcast.55, f32[]{:T(128)} %bitcast.54, ...), kind=kLoop, calls=%fused_computation.671 | loop fusion | flops 819200 | bytes 196708 | tf_op jit(solution)/shard_map/mul | solution.py:79
  374.3 11.4 %broadcast_multiply_fusion.44 = (f32[128,128]{1,0:T(8,128)S(1)}, f32[128,128]{1,0:T(8,128)S(1)}, f32[128,128]{1,0:T(8,128)S(1)}, f32[128,128]{1,0:T(8,128)S(1)},...) fusion(f32[128,128]{1,0:T(8,128)S(1)} %get-tuple-element.36, ...), kind=kLoop, calls=%fused_computation.669 | loop fusion | flops 294912 | bytes 1245256 | tf_op jit(solution)/shard_map/mul | solution.py:79
  390.7 64.1 %all-reduce.103 = (f32[32,1,3,3]{0,1,3,2:T(1,128)}, f32[32,32,3,3]{1,0,3,2:T(8,128)}, f32[1,32,3,3]{1,0,3,2:T(1,128)}) all-reduce(f32[32,1,3,3]{0,1,3,2:T(1,128)S(1)} %maximum_multiply_fusion.1, f32[32,32,3,3]{1,0,3,2:T(8,128)S(1)} %copy-done.14, ...), channel_id=1, replica_groups=mesh['parts'=2,'rows'=16] {'rows'}, use_global_device_ids=true, to_apply=%region_1.2 | all-reduce | flops 9792 | bytes 78336 | tf_op jit(solution)/shard_map/psum | solution.py:166
  (332 shorter events, 142.1 us)
Async XLA Ops:
  0.6 139.5 %copy-start = (bf16[32,32,3,3]{1,0,3,2:T(8,128)(2,1)S(1)}, bf16[32,32,3,3]{1,0,3,2:T(8,128)(2,1)}, u32[]{:S(2)}) copy-start(bf16[32,32,3,3]{1,0,3,2:T(8,128)(2,1)} %param.16) | copy-start | bytes 55300
  1.5 64.8 %collective-permute-start.6 = (bf16[1,1,2048]{2,1,0:T(2,128)(2,1)S(1)}, bf16[1,1,2048]{2,1,0:T(2,128)(2,1)S(1)}, u32[]{:S(2)}, u32[]{:S(2)}) collective-permute-start(bf16[1,1,2048]{2,1,0:T(2,128)(2,1)S(1)} %get-tuple-element.165), channel_id=1, source_target_pairs={{0,1},{1,2},{2,3},{3,4},{4,5},{5,6},{6,7},{7,8},{8,9},{9,10},{10,1... | collective-permute-start | bytes 12296 | tf_op jit(solution)/shard_map/ppermute | solution.py:20
  3.9 62.4 %collective-permute-start.7 = (bf16[1,1,2048]{2,1,0:T(2,128)(2,1)S(1)}, bf16[1,1,2048]{2,1,0:T(2,128)(2,1)S(1)}, u32[]{:S(2)}, u32[]{:S(2)}) collective-permute-start(bf16[1,1,2048]{2,1,0:T(2,128)(2,1)S(1)} %get-tuple-element.166), channel_id=1, source_target_pairs={{1,0},{2,1},{3,2},{4,3},{5,4},{6,5},{7,6},{8,7},{9,8},{10,9},{11,1... | collective-permute-start | bytes 12296 | tf_op jit(solution)/shard_map/ppermute | solution.py:21
  8.6 64.7 %copy-start.17 = (f32[2048]{0:T(1024)}, f32[2048]{0:T(1024)S(1)}, u32[]{:S(2)}) copy-start(f32[2048]{0:T(1024)S(1)} %broadcast_bitcast_fusion.24) | copy-start | bytes 24580
  8.7 64.6 %copy-start.19 = (f32[2048]{0:T(1024)}, f32[2048]{0:T(1024)S(1)}, u32[]{:S(2)}) copy-start(f32[2048]{0:T(1024)S(1)} %get-tuple-element.216) | copy-start | bytes 24580
  8.7 64.6 %copy-start.21 = (f32[2048]{0:T(1024)}, f32[2048]{0:T(1024)S(1)}, u32[]{:S(2)}) copy-start(f32[2048]{0:T(1024)S(1)} %get-tuple-element.217) | copy-start | bytes 24580
  8.7 64.5 %copy-start.39 = (f32[2048]{0:T(1024)}, f32[2048]{0:T(1024)S(1)}, u32[]{:S(2)}) copy-start(f32[2048]{0:T(1024)S(1)} %get-tuple-element.194) | copy-start | bytes 24580
  8.7 64.5 %copy-start.41 = (f32[2048]{0:T(1024)}, f32[2048]{0:T(1024)S(1)}, u32[]{:S(2)}) copy-start(f32[2048]{0:T(1024)S(1)} %get-tuple-element.195) | copy-start | bytes 24580
  8.8 64.4 %copy-start.47 = (f32[2048]{0:T(1024)}, f32[2048]{0:T(1024)S(1)}, u32[]{:S(2)}) copy-start(f32[2048]{0:T(1024)S(1)} %get-tuple-element.196) | copy-start | bytes 24580
  8.8 64.4 %copy-start.49 = (f32[2048]{0:T(1024)}, f32[2048]{0:T(1024)S(1)}, u32[]{:S(2)}) copy-start(f32[2048]{0:T(1024)S(1)} %get-tuple-element.197) | copy-start | bytes 24580
  8.9 64.3 %copy-start.55 = (f32[2048]{0:T(1024)}, f32[2048]{0:T(1024)S(1)}, u32[]{:S(2)}) copy-start(f32[2048]{0:T(1024)S(1)} %get-tuple-element.198) | copy-start | bytes 24580
  8.9 64.3 %copy-start.57 = (f32[2048]{0:T(1024)}, f32[2048]{0:T(1024)S(1)}, u32[]{:S(2)}) copy-start(f32[2048]{0:T(1024)S(1)} %get-tuple-element.199) | copy-start | bytes 24580
  9.0 64.4 %copy-start.25 = (f32[2048]{0:T(1024)}, f32[2048]{0:T(1024)S(1)}, u32[]{:S(2)}) copy-start(f32[2048]{0:T(1024)S(1)} %get-tuple-element.200) | copy-start | bytes 24580
  9.0 64.4 %copy-start.27 = (f32[2048]{0:T(1024)}, f32[2048]{0:T(1024)S(1)}, u32[]{:S(2)}) copy-start(f32[2048]{0:T(1024)S(1)} %get-tuple-element.201) | copy-start | bytes 24580
  9.0 64.3 %copy-start.29 = (f32[2048]{0:T(1024)}, f32[2048]{0:T(1024)S(1)}, u32[]{:S(2)}) copy-start(f32[2048]{0:T(1024)S(1)} %get-tuple-element.202) | copy-start | bytes 24580
  9.0 64.3 %copy-start.31 = (f32[2048]{0:T(1024)}, f32[2048]{0:T(1024)S(1)}, u32[]{:S(2)}) copy-start(f32[2048]{0:T(1024)S(1)} %get-tuple-element.203) | copy-start | bytes 24580
  9.1 64.3 %copy-start.35 = (f32[2048]{0:T(1024)}, f32[2048]{0:T(1024)S(1)}, u32[]{:S(2)}) copy-start(f32[2048]{0:T(1024)S(1)} %get-tuple-element.205) | copy-start | bytes 24580
  9.2 64.4 %copy-start.23 = (f32[2048]{0:T(1024)}, f32[2048]{0:T(1024)S(1)}, u32[]{:S(2)}) copy-start(f32[2048]{0:T(1024)S(1)} %get-tuple-element.206) | copy-start | bytes 24580
  13.1 16.2 %all-to-all-start = ((f32[8,16,128]{2,0,1:T(8,128)}), f32[8,16,128]{2,0,1:T(8,128)S(1)}, u32[]{:S(2)}, u32[]{:S(2)}) async-start(f32[8,16,128]{2,0,1:T(8,128)} %add_bitcast_fusion.1), calls=%async_computation | async-start | bytes 131072 | tf_op jit(solution)/shard_map/all_to_all | solution.py:111
  62.2 11.0 %all-to-all-start.1 = ((f32[16,8,128]{2,1,0:T(8,128)}), f32[16,8,128]{2,1,0:T(8,128)S(1)}, u32[]{:S(2)}, u32[]{:S(2)}) async-start(f32[16,8,128]{2,1,0:T(8,128)} %fusion.342), calls=%async_computation.1 | async-start | bytes 131072 | tf_op jit(solution)/shard_map/all_to_all | solution.py:116
  74.8 18.0 %collective-permute-start = (bf16[1,1,2048]{2,1,0:T(2,128)(2,1)S(1)}, bf16[1,1,2048]{2,1,0:T(2,128)(2,1)S(1)}, u32[]{:S(2)}, u32[]{:S(2)}) collective-permute-start(bf16[1,1,2048]{2,1,0:T(2,128)(2,1)S(1)} %get-tuple-element.167), channel_id=1, source_target_pairs={{0,1},{1,2},{2,3},{3,4},{4,5},{5,6},{6,7},{7,8},{8,9},{9,10},{10,1... | collective-permute-start | bytes 12296 | tf_op jit(solution)/shard_map/ppermute | solution.py:20
  76.2 16.5 %collective-permute-start.1 = (bf16[1,1,2048]{2,1,0:T(2,128)(2,1)S(1)}, bf16[1,1,2048]{2,1,0:T(2,128)(2,1)S(1)}, u32[]{:S(2)}, u32[]{:S(2)}) collective-permute-start(bf16[1,1,2048]{2,1,0:T(2,128)(2,1)S(1)} %get-tuple-element.168), channel_id=1, source_target_pairs={{1,0},{2,1},{3,2},{4,3},{5,4},{6,5},{7,6},{8,7},{9,8},{10,9},{11,1... | collective-permute-start | bytes 12296 | tf_op jit(solution)/shard_map/ppermute | solution.py:21
  117.3 5.2 %collective-permute-start.2 = (bf16[32,1,2048]{2,0,1:T(8,128)(2,1)S(1)}, bf16[32,1,2048]{2,0,1:T(8,128)(2,1)S(1)}, u32[]{:S(2)}, u32[]{:S(2)}) collective-permute-start(bf16[32,1,2048]{2,0,1:T(8,128)(2,1)S(1)} %get-tuple-element.57), channel_id=1, source_target_pairs={{0,1},{1,2},{2,3},{3,4},{4,5},{5,6},{6,7},{7,8},{8,9},{9,10},{10,1... | collective-permute-start | bytes 393224 | tf_op jit(solution)/shard_map/ppermute | solution.py:20
  120.6 4.5 collective-permute-start.3
  196.1 18.9 %collective-permute-start.4 = (bf16[32,1,2048]{2,0,1:T(8,128)(2,1)}, bf16[32,1,2048]{2,0,1:T(8,128)(2,1)}, u32[]{:S(2)}, u32[]{:S(2)}) collective-permute-start(bf16[32,1,2048]{2,0,1:T(8,128)(2,1)} %get-tuple-element.55), channel_id=1, source_target_pairs={{0,1},{1,2},{2,3},{3,4},{4,5},{5,6},{6,7},{7,8},{8,9},{9,10},{10,1... | collective-permute-start | bytes 393224 | tf_op jit(solution)/shard_map/ppermute | solution.py:20
  202.2 12.8 %collective-permute-start.5 = (bf16[32,1,2048]{2,0,1:T(8,128)(2,1)}, bf16[32,1,2048]{2,0,1:T(8,128)(2,1)}, u32[]{:S(2)}, u32[]{:S(2)}) collective-permute-start(bf16[32,1,2048]{2,0,1:T(8,128)(2,1)} %get-tuple-element.56), channel_id=1, source_target_pairs={{1,0},{2,1},{3,2},{4,3},{5,4},{6,5},{7,6},{8,7},{9,8},{10,9},{11,1... | collective-permute-start | bytes 393224 | tf_op jit(solution)/shard_map/ppermute | solution.py:21
  203.5 7.0 %collective-permute-start.8 = (bf16[32,1,2048]{2,0,1:T(8,128)(2,1)}, bf16[32,1,2048]{2,0,1:T(8,128)(2,1)S(1)}, u32[]{:S(2)}, u32[]{:S(2)}) collective-permute-start(bf16[32,1,2048]{2,0,1:T(8,128)(2,1)} %get-tuple-element.53), channel_id=1, source_target_pairs={{0,1},{1,2},{2,3},{3,4},{4,5},{5,6},{6,7},{7,8},{8,9},{9,10},{10,1... | collective-permute-start | bytes 393224 | tf_op jit(solution)/shard_map/ppermute | solution.py:20
  206.5 5.0 %collective-permute-start.9 = (bf16[32,1,2048]{2,0,1:T(8,128)(2,1)S(1)}, bf16[32,1,2048]{2,0,1:T(8,128)(2,1)S(1)}, u32[]{:S(2)}, u32[]{:S(2)}) collective-permute-start(bf16[32,1,2048]{2,0,1:T(8,128)(2,1)S(1)} %get-tuple-element.54), channel_id=1, source_target_pairs={{1,0},{2,1},{3,2},{4,3},{5,4},{6,5},{7,6},{8,7},{9,8},{10,9},{11,1... | collective-permute-start | bytes 393224 | tf_op jit(solution)/shard_map/ppermute | solution.py:21
  297.8 7.9 %collective-permute-start.10 = (bf16[32,1,2048]{2,0,1:T(8,128)(2,1)S(1)}, bf16[32,1,2048]{2,0,1:T(8,128)(2,1)S(1)}, u32[]{:S(2)}, u32[]{:S(2)}) collective-permute-start(bf16[32,1,2048]{2,0,1:T(8,128)(2,1)S(1)} %get-tuple-element.51), channel_id=1, source_target_pairs={{0,1},{1,2},{2,3},{3,4},{4,5},{5,6},{6,7},{7,8},{8,9},{9,10},{10,1... | collective-permute-start | bytes 393224 | tf_op jit(solution)/shard_map/ppermute | solution.py:20
  303.3 3.2 collective-permute-start.11
  339.3 15.8 %all-to-all-start.2 = ((f32[8,16,128]{2,0,1:T(8,128)}), f32[8,16,128]{2,0,1:T(8,128)S(1)}, u32[]{:S(2)}, u32[]{:S(2)}) async-start(f32[8,16,128]{2,0,1:T(8,128)} %add_bitcast_fusion), calls=%async_computation.2 | async-start | bytes 131072 | tf_op jit(solution)/shard_map/all_to_all | solution.py:111
  387.1 67.7 %all-to-all-start.3 = ((f32[16,8,128]{2,1,0:T(8,128)}), f32[16,8,128]{2,1,0:T(8,128)S(1)}, u32[]{:S(2)}, u32[]{:S(2)}) async-start(f32[16,8,128]{2,1,0:T(8,128)} %fusion.341), calls=%async_computation.3 | async-start | bytes 131072 | tf_op jit(solution)/shard_map/all_to_all | solution.py:116
  (68 other events, 889.4 us)
where the time goes:
time: 463 us; the launch traced here: 456 us
  local copies, waits for them, and re-layouts  139 us (30%)
  other arithmetic  99.6 us (22%)
  matrix products  80.2 us (17%)
  blocking collectives  64.1 us (14%)
  starting transfers between devices  55.6 us (12%)
  waiting for transfers between devices  15.9 us (3%)
    conv_general_dilated x34, local copies, waits for them, and re-layouts, conv_rim(): lax.conv_general_dilated(padded[None], weight, (1, 1), padding, dimension...  116 us
    psum x1, blocking collectives, on_device(): lax.psum((partial_grads[0] * grad_scale, partial_grads[1] * grad_scale, p...  64.1 us
    mul x10, other arithmetic, blur_line(): spread = jnp.pad(factor * values, widths)  62.5 us
    conv_general_dilated x6, matrix products, conv_rim(): lax.conv_general_dilated(padded[None], weight, (1, 1), padding, dimension...  61 us
    ppermute x6, starting transfers between devices, padded_2(): before = lax.ppermute(last, axis, up)  21.6 us
    all_to_all x2, starting transfers between devices, data_gradient(): lax.all_to_all(blurred, 'rows', split_axis=1, concat_axis=0, tiled=True)  18.1 us
    dot_general x27, matrix products, weight_taps(): jnp.einsum('ohw,chw->oc', errors, window, preferred_element_type=jnp.floa...  16.8 us
    convert_element_type x2, other arithmetic, denoise(): (conv_rim(cot_pad, flipped(w_last)) * silu_slope(pre_mid)).astype(jnp.bfl...  10.5 us
  transfers between devices with their start and end apart: 16, of which 6 were waited for; matrix products, arithmetic and copies ran while one was open for 16% of the time, Pallas kernels for 0%

commit v1 on v0

--- a/solution.py
+++ b/solution.py
@@ -108,7 +108,10 @@
 
 def data_gradient(values, target, row_coef, col_coef):
     blurred = blur_line(values, row_coef, 1, False)
-    columns = lax.all_to_all(blurred, "rows", split_axis=1, concat_axis=0, tiled=True)
+    columns = jnp.concatenate(
+        lax.all_to_all(jnp.stack(jnp.split(blurred, lax.axis_size("rows"), axis=1)), "rows", 0, 0),
+        axis=0,
+    )
     columns = blur_line(columns, col_coef, 0, False)
     if target is not None:
         columns = columns - target

time: 463 us -> 481 us (1.039)
  local copies, waits for them, and re-layouts: 139 us -> 158 us
    unnamed x168 -> x198, local copies, waits for them, and re-layouts: 2.41 us -> 20.2 us
  transfers between devices with their start and end apart: 16 -> 16, of which waited for: 6 -> 6; matrix products, arithmetic and copies ran while one was open for 16% -> 17% of each run, Pallas kernels for 0% -> 0%
where the time goes in v1:
time: 481 us; the launch traced here: 474 us
  local copies, waits for them, and re-layouts  158 us (33%)
  other arithmetic  98.4 us (20%)
  matrix products  80.2 us (17%)
  blocking collectives  64.1 us (13%)
  starting transfers between devices  55.6 us (12%)
  waiting for transfers between devices  15.9 us (3%)
    conv_general_dilated x34, local copies, waits for them, and re-layouts, conv_rim(): lax.conv_general_dilated(padded[None], weight, (1, 1), padding, dimension...  116 us
    psum x1, blocking collectives, on_device(): lax.psum((partial_grads[0] * grad_scale, partial_grads[1] * grad_scale, p...  64.1 us
    mul x10, other arithmetic, blur_line(): spread = jnp.pad(factor * values, widths)  62.5 us
    conv_general_dilated x6, matrix products, conv_rim(): lax.conv_general_dilated(padded[None], weight, (1, 1), padding, dimension...  61 us
    ppermute x6, starting transfers between devices, padded_2(): before = lax.ppermute(last, axis, up)  21.6 us
    unnamed x198, local copies, waits for them, and re-layouts  20.2 us
    all_to_all x2, starting transfers between devices, data_gradient(): lax.all_to_all(jnp.stack(jnp.split(blurred, lax.axis_size('rows'), axis=1...  18.1 us
    dot_general x27, matrix products, weight_taps(): jnp.einsum('ohw,chw->oc', errors, window, preferred_element_type=jnp.floa...  16.8 us
  transfers between devices with their start and end apart: 16, of which 6 were waited for; matrix products, arithmetic and copies ran while one was open for 17% of the time, Pallas kernels for 0%

profile of v1, /device:TPU:0, one launch (start us, length us, event | category | flops | bytes accessed | tf_op | source)
XLA Modules:
  0.0 474.2 jit_solution(439270120725951630)
XLA Ops:
  22.0 9.3 %all-to-all-start = ((f32[16,8,128]{2,1,0:T(8,128)}), f32[16,8,128]{2,1,0:T(8,128)S(1)}, u32[]{:S(2)}, u32[]{:S(2)}) async-start(f32[16,8,128]{2,1,0:T(8,128)} %constant_dynamic-update-slice_fusion), calls=%async_computation | async-start | bytes 131072 | tf_op jit(solution)/shard_map/all_to_all | solution.py:112
  38.2 16.7 %broadcast_multiply_fusion.47 = (f32[128,128]{1,0:T(8,128)S(1)}, f32[128,128]{1,0:T(8,128)S(1)}) fusion(f32[]{:T(128)} %bitcast.9, f32[128,128]{1,0:T(8,128)} %param.10, f32[]{:T(128)} %bitcast.74, f32[]{:T(128)} %bitcast.73, f32[]{:T(128)} %bitcast.72, f32[]{:T(128)} %bitcast.71, f32[]{:T(128)} %bitcast.70, f32[]{:T(128)} %bitcast.69, f32[]{:T(128)} %bitcast.68, ...), kind=kLoop, calls=%fused_computation.704 | loop fusion | flops 835584 | bytes 262244 | tf_op jit(solution)/shard_map/mul | solution.py:79
  58.2 11.4 %broadcast_multiply_fusion.45 = (f32[128,128]{1,0:T(8,128)S(1)}, f32[128,128]{1,0:T(8,128)S(1)}, f32[128,128]{1,0:T(8,128)S(1)}, f32[128,128]{1,0:T(8,128)S(1)},...) fusion(f32[128,128]{1,0:T(8,128)S(1)} %get-tuple-element.38, ...), kind=kLoop, calls=%fused_computation.702 | loop fusion | flops 294912 | bytes 1245256 | tf_op jit(solution)/shard_map/mul | solution.py:79
  76.8 5.3 %all-to-all-done.1 = f32[16,8,128]{2,1,0:T(8,128)S(1)} async-done(((f32[16,8,128]{2,1,0:T(8,128)}), f32[16,8,128]{2,1,0:T(8,128)S(1)}, u32[]{:S(2)}, u32[]{:S(2)}) %all-to-all-start.1) | async-done | bytes 65568 | tf_op jit(solution)/shard_map/all_to_all | solution.py:119
  86.9 7.6 %fusion.358 = f32[8,8,257,32]{3,1,2,0:T(8,128)} fusion(bf16[1,10,8,259]{2,0,3,1:T(2,128)(2,1)S(1)} %copy.104, bf16[32,1,3,3]{0,3,2,1:T(4,128)(2,1)S(1)} %bitcast.591), kind=kOutput, calls=%fused_computation.741 | convolution fusion | flops 9474048 | bytes 2147360 | tf_op jit(solution)/shard_map/conv_general_dilated | solution.py:37
  94.5 7.2 %copy.106 = f32[8,8,257,32]{2,3,1,0:T(8,128)} copy(f32[8,8,257,32]{3,1,2,0:T(8,128)} %fusion.358) | data formatting | bytes 4210688 | tf_op jit(solution)/shard_map/conv_general_dilated | solution.py:37
  104.0 7.6 %fusion.361 = f32[8,8,257,32]{3,1,2,0:T(8,128)} fusion(bf16[1,10,8,259]{2,0,3,1:T(2,128)(2,1)S(1)} %copy.92, bf16[32,1,3,3]{0,3,2,1:T(4,128)(2,1)S(1)} %copy-done.80), kind=kOutput, calls=%fused_computation.744 | convolution fusion | flops 9474048 | bytes 2147360 | tf_op jit(solution)/shard_map/conv_general_dilated | solution.py:37
  111.6 5.9 %copy.94 = f32[8,8,257,32]{2,3,1,0:T(8,128)S(1)} copy(f32[8,8,257,32]{3,1,2,0:T(8,128)} %fusion.361) | data formatting | bytes 4210688 | tf_op jit(solution)/shard_map/conv_general_dilated | solution.py:37
  135.8 4.9 %reshape.470 = bf16[32,10,1,8,257]{4,3,0,1,2:T(8,128)(2,1)} reshape(bf16[32,10,1,2056]{3,0,1,2:T(8,128)(2,1)} %pad.422) | data formatting | bytes 2631680 | tf_op jit(solution)/shard_map/conv_general_dilated | solution.py:37
  140.7 7.5 %copy.97 = bf16[32,10,1,8,257]{0,3,4,1,2:T(8,128)(2,1)} copy(bf16[32,10,1,8,257]{4,3,0,1,2:T(8,128)(2,1)} %reshape.470) | data formatting | bytes 2631680 | tf_op jit(solution)/shard_map/conv_general_dilated | solution.py:37
  149.0 11.1 %fusion.6 = f32[8,8,257,32]{3,1,2,0:T(8,128)} fusion(bf16[32,32,3,3]{1,0,3,2:T(8,128)(2,1)S(1)} %copy-done, bf16[32,10,1,7,2]{0,3,4,1,2:T(8,128)(2,1)S(1)} %slice.1495, bf16[32,10,1,8,257]{0,3,4,1,2:T(8,128)(2,1)} %copy.97), kind=kOutput, calls=%fused_computation.7 | convolution fusion | flops 307147776 | bytes 3448576 | tf_op jit(solution)/shard_map/conv_general_dilated | solution.py:37
  160.1 7.1 %copy.98 = f32[8,8,257,32]{2,3,1,0:T(8,128)} copy(f32[8,8,257,32]{3,1,2,0:T(8,128)} %fusion.6) | data formatting | bytes 4210688 | tf_op jit(solution)/shard_map/conv_general_dilated | solution.py:37
  167.2 6.4 %multiply_convert_fusion.1 = (bf16[8,8,257,32]{2,3,1,0:T(8,128)(2,1)}, f32[8,8,257,32]{2,3,1,0:T(8,128)S(1)}, f32[8,8,257,32]{2,3,1,0:T(8,128)}) fusion(f32[8,8,257,32]{2,3,1,0:T(8,128)} %copy.98, pred[8,257]{1,0:T(8,128)(4,1)S(1)} %copy-done.79, f32[8,8,257,32]{2,3,1,0:T(8,128)} %copy.106), kind=kLoop, calls=%fused_computation.32 | loop fusion | flops 5789696 | bytes 9476104 | tf_op jit(solution)/shard_map/convert_element_type | solution.py:139
  181.2 5.3 %copy.99 = f32[8,8,257,32]{2,1,3,0:T(8,128)} copy(f32[8,8,257,32]{2,3,1,0:T(8,128)} %get-tuple-element.41) | data formatting | bytes 4210688 | tf_op jit(solution)/shard_map/conv_general_dilated | solution.py:37
  186.5 4.4 reshape.474
  204.9 6.1 %collective-permute-start.4 = (bf16[32,1,2048]{2,0,1:T(8,128)(2,1)}, bf16[32,1,2048]{2,0,1:T(8,128)(2,1)}, u32[]{:S(2)}, u32[]{:S(2)}) collective-permute-start(bf16[32,1,2048]{2,0,1:T(8,128)(2,1)} %get-tuple-element.55), channel_id=1, source_target_pairs={{0,1},{1,2},{2,3},{3,4},{4,5},{5,6},{6,7},{7,8},{8,9},{9,10},{10,1... | collective-permute-start | bytes 393224 | tf_op jit(solution)/shard_map/ppermute | solution.py:20
  230.3 7.5 %copy.101 = bf16[32,10,1,8,257]{0,3,4,1,2:T(8,128)(2,1)} copy(bf16[32,10,1,8,257]{4,3,0,1,2:T(8,128)(2,1)} %reshape.477) | data formatting | bytes 2631680 | tf_op jit(solution)/shard_map/conv_general_dilated | solution.py:37
  238.6 11.8 %broadcast_select_fusion.1 = f32[8,8,257,1]{3,1,2,0:T(8,128)} fusion(pred[8,257]{0,1:T(8,128)(4,1)S(1)} %copy-done.82, bf16[32,10,1,7,2]{0,3,4,1,2:T(8,128)(2,1)S(1)} %slice.1499, bf16[32,10,1,8,257]{0,3,4,1,2:T(8,128)(2,1)} %copy.101, bf16[1,32,3,3]{1,3,2,0:T(4,128)(2,1)S(1)} %copy-done.81), kind=kOutput, calls=%fused_computation.30 | convolution fusion | flops 13468736 | bytes 1393224 | tf_op jit(solution)/shard_map/conv_general_dilated | solution.py:37
  250.4 6.1 %copy.103 = f32[8,8,257,1]{2,1,0,3:T(8,128)S(1)} copy(f32[8,8,257,1]{3,1,2,0:T(8,128)} %broadcast_select_fusion.1) | data formatting | bytes 131584 | tf_op jit(solution)/shard_map/conv_general_dilated | solution.py:37
  257.3 5.3 %copy.109 = bf16[32,10,1,8,257]{0,3,4,1,2:T(8,128)(2,1)} copy(bf16[32,10,1,8,257]{4,3,0,1,2:T(8,128)(2,1)S(1)} %reshape.493) | data formatting | bytes 2631680 | tf_op jit(solution)/shard_map/conv_general_dilated | solution.py:37
  263.4 11.2 %fusion.14 = f32[8,8,257,32]{3,1,2,0:T(8,128)} fusion(bf16[32,32,3,3]{1,0,3,2:T(8,128)(2,1)S(1)} %copy-done, bf16[32,10,1,7,2]{0,3,4,1,2:T(8,128)(2,1)S(1)} %slice.1507, bf16[32,10,1,8,257]{0,3,4,1,2:T(8,128)(2,1)} %copy.109), kind=kOutput, calls=%fused_computation.13 | convolution fusion | flops 307147776 | bytes 3448576 | tf_op jit(solution)/shard_map/conv_general_dilated | solution.py:37
  274.6 7.3 %copy.110 = f32[8,8,257,32]{2,3,1,0:T(8,128)} copy(f32[8,8,257,32]{3,1,2,0:T(8,128)} %fusion.14) | data formatting | bytes 4210688 | tf_op jit(solution)/shard_map/conv_general_dilated | solution.py:37
  281.8 5.6 %multiply_convert_fusion.2 = (bf16[8,8,257,32]{2,3,1,0:T(8,128)(2,1)S(1)}, bf16[8,8,257,32]{2,3,1,0:T(8,128)(2,1)}, f32[8,8,257,32]{2,3,1,0:T(8,128)}) fusion(f32[8,8,257,32]{2,3,1,0:T(8,128)S(1)} %copy-done.2, pred[8,257]{1,0:T(8,128)(4,1)S(1)} %copy-done.79, f32[8,8,257,32]{2,3,1,0:T(8,128)} %copy.110), kind=kLoop, calls=%fused_computation.33 | loop fusion | flops 6842368 | bytes 8423432 | tf_op jit(solution)/shard_map/convert_element_type | solution.py:131
  299.8 4.3 reshape.497
  306.7 5.5 %collective-permute-start.10 = (bf16[32,1,2048]{2,0,1:T(8,128)(2,1)S(1)}, bf16[32,1,2048]{2,0,1:T(8,128)(2,1)S(1)}, u32[]{:S(2)}, u32[]{:S(2)}) collective-permute-start(bf16[32,1,2048]{2,0,1:T(8,128)(2,1)S(1)} %get-tuple-element.51), channel_id=1, source_target_pairs={{0,1},{1,2},{2,3},{3,4},{4,5},{5,6},{6,7},{7,8},{8,9},{9,10},{10,1... | collective-permute-start | bytes 393224 | tf_op jit(solution)/shard_map/ppermute | solution.py:20
  318.7 5.2 %copy.113 = bf16[32,10,1,8,257]{0,3,4,1,2:T(8,128)(2,1)} copy(bf16[32,10,1,8,257]{4,3,0,1,2:T(8,128)(2,1)S(1)} %reshape.502) | data formatting | bytes 2631680 | tf_op jit(solution)/shard_map/conv_general_dilated | solution.py:37
  324.7 11.8 %broadcast_select_fusion = f32[8,8,257,1]{3,1,2,0:T(8,128)} fusion(pred[8,257]{0,1:T(8,128)(4,1)S(1)} %copy-done.83, bf16[32,10,1,7,2]{0,3,4,1,2:T(8,128)(2,1)S(1)} %slice.1511, bf16[32,10,1,8,257]{0,3,4,1,2:T(8,128)(2,1)} %copy.113, bf16[1,32,3,3]{1,3,2,0:T(4,128)(2,1)S(1)} %bitcast.590), kind=kOutput, calls=%fused_computation.29 | convolution fusion | flops 13468736 | bytes 1393224 | tf_op jit(solution)/shard_map/conv_general_dilated | solution.py:37
  336.5 6.3 %copy.115 = f32[8,8,257,1]{2,1,0,3:T(8,128)S(1)} copy(f32[8,8,257,1]{3,1,2,0:T(8,128)} %broadcast_select_fusion) | data formatting | bytes 131584 | tf_op jit(solution)/shard_map/conv_general_dilated | solution.py:37
  357.1 8.8 %all-to-all-start.2 = ((f32[16,8,128]{2,1,0:T(8,128)}), f32[16,8,128]{2,1,0:T(8,128)S(1)}, u32[]{:S(2)}, u32[]{:S(2)}) async-start(f32[16,8,128]{2,1,0:T(8,128)} %constant_dynamic-update-slice_fusion.16), calls=%async_computation.2 | async-start | bytes 131072 | tf_op jit(solution)/shard_map/all_to_all | solution.py:112
  372.9 15.9 %broadcast_multiply_fusion.46 = (f32[128,128]{1,0:T(8,128)S(1)}, f32[128,128]{1,0:T(8,128)S(1)}) fusion(f32[]{:T(128)} %bitcast.9, f32[]{:T(128)} %bitcast.74, f32[]{:T(128)} %bitcast.73, f32[]{:T(128)} %bitcast.72, f32[]{:T(128)} %bitcast.71, f32[]{:T(128)} %bitcast.70, f32[]{:T(128)} %bitcast.69, f32[]{:T(128)} %bitcast.68, f32[]{:T(128)} %bitcast.67, ...), kind=kLoop, calls=%fused_computation.703 | loop fusion | flops 819200 | bytes 196708 | tf_op jit(solution)/shard_map/mul | solution.py:79
  392.1 11.4 %broadcast_multiply_fusion.44 = (f32[128,128]{1,0:T(8,128)S(1)}, f32[128,128]{1,0:T(8,128)S(1)}, f32[128,128]{1,0:T(8,128)S(1)}, f32[128,128]{1,0:T(8,128)S(1)},...) fusion(f32[128,128]{1,0:T(8,128)S(1)} %get-tuple-element.36, ...), kind=kLoop, calls=%fused_computation.701 | loop fusion | flops 294912 | bytes 1245256 | tf_op jit(solution)/shard_map/mul | solution.py:79
  408.5 64.1 %all-reduce.103 = (f32[32,1,3,3]{0,1,3,2:T(1,128)}, f32[32,32,3,3]{1,0,3,2:T(8,128)}, f32[1,32,3,3]{1,0,3,2:T(1,128)}) all-reduce(f32[32,1,3,3]{0,1,3,2:T(1,128)S(1)} %maximum_multiply_fusion.1, f32[32,32,3,3]{1,0,3,2:T(8,128)S(1)} %copy-done.14, ...), channel_id=1, replica_groups=mesh['parts'=2,'rows'=16] {'rows'}, use_global_device_ids=true, to_apply=%region_1.2 | all-reduce | flops 9792 | bytes 78336 | tf_op jit(solution)/shard_map/psum | solution.py:169
  (364 shorter events, 159.9 us)
Async XLA Ops:
  0.6 148.4 %copy-start = (bf16[32,32,3,3]{1,0,3,2:T(8,128)(2,1)S(1)}, bf16[32,32,3,3]{1,0,3,2:T(8,128)(2,1)}, u32[]{:S(2)}) copy-start(bf16[32,32,3,3]{1,0,3,2:T(8,128)(2,1)} %param.16) | copy-start | bytes 55300
  1.5 73.6 %collective-permute-start.6 = (bf16[1,1,2048]{2,1,0:T(2,128)(2,1)S(1)}, bf16[1,1,2048]{2,1,0:T(2,128)(2,1)S(1)}, u32[]{:S(2)}, u32[]{:S(2)}) collective-permute-start(bf16[1,1,2048]{2,1,0:T(2,128)(2,1)S(1)} %get-tuple-element.165), channel_id=1, source_target_pairs={{0,1},{1,2},{2,3},{3,4},{4,5},{5,6},{6,7},{7,8},{8,9},{9,10},{10,1... | collective-permute-start | bytes 12296 | tf_op jit(solution)/shard_map/ppermute | solution.py:20
  3.9 71.3 %collective-permute-start.7 = (bf16[1,1,2048]{2,1,0:T(2,128)(2,1)S(1)}, bf16[1,1,2048]{2,1,0:T(2,128)(2,1)S(1)}, u32[]{:S(2)}, u32[]{:S(2)}) collective-permute-start(bf16[1,1,2048]{2,1,0:T(2,128)(2,1)S(1)} %get-tuple-element.166), channel_id=1, source_target_pairs={{1,0},{2,1},{3,2},{4,3},{5,4},{6,5},{7,6},{8,7},{9,8},{10,9},{11,1... | collective-permute-start | bytes 12296 | tf_op jit(solution)/shard_map/ppermute | solution.py:21
  8.6 73.6 %copy-start.17 = (f32[2048]{0:T(1024)}, f32[2048]{0:T(1024)S(1)}, u32[]{:S(2)}) copy-start(f32[2048]{0:T(1024)S(1)} %broadcast_bitcast_fusion.24) | copy-start | bytes 24580
  8.7 73.5 %copy-start.19 = (f32[2048]{0:T(1024)}, f32[2048]{0:T(1024)S(1)}, u32[]{:S(2)}) copy-start(f32[2048]{0:T(1024)S(1)} %get-tuple-element.216) | copy-start | bytes 24580
  8.7 73.5 %copy-start.21 = (f32[2048]{0:T(1024)}, f32[2048]{0:T(1024)S(1)}, u32[]{:S(2)}) copy-start(f32[2048]{0:T(1024)S(1)} %get-tuple-element.217) | copy-start | bytes 24580
  8.7 73.3 %copy-start.39 = (f32[2048]{0:T(1024)}, f32[2048]{0:T(1024)S(1)}, u32[]{:S(2)}) copy-start(f32[2048]{0:T(1024)S(1)} %get-tuple-element.194) | copy-start | bytes 24580
  8.7 73.3 %copy-start.41 = (f32[2048]{0:T(1024)}, f32[2048]{0:T(1024)S(1)}, u32[]{:S(2)}) copy-start(f32[2048]{0:T(1024)S(1)} %get-tuple-element.195) | copy-start | bytes 24580
  8.8 73.3 %copy-start.47 = (f32[2048]{0:T(1024)}, f32[2048]{0:T(1024)S(1)}, u32[]{:S(2)}) copy-start(f32[2048]{0:T(1024)S(1)} %get-tuple-element.196) | copy-start | bytes 24580
  8.8 73.3 %copy-start.49 = (f32[2048]{0:T(1024)}, f32[2048]{0:T(1024)S(1)}, u32[]{:S(2)}) copy-start(f32[2048]{0:T(1024)S(1)} %get-tuple-element.197) | copy-start | bytes 24580
  8.9 73.2 %copy-start.55 = (f32[2048]{0:T(1024)}, f32[2048]{0:T(1024)S(1)}, u32[]{:S(2)}) copy-start(f32[2048]{0:T(1024)S(1)} %get-tuple-element.198) | copy-start | bytes 24580
  8.9 73.2 %copy-start.57 = (f32[2048]{0:T(1024)}, f32[2048]{0:T(1024)S(1)}, u32[]{:S(2)}) copy-start(f32[2048]{0:T(1024)S(1)} %get-tuple-element.199) | copy-start | bytes 24580
  9.0 73.2 %copy-start.25 = (f32[2048]{0:T(1024)}, f32[2048]{0:T(1024)S(1)}, u32[]{:S(2)}) copy-start(f32[2048]{0:T(1024)S(1)} %get-tuple-element.200) | copy-start | bytes 24580
  9.0 73.2 %copy-start.27 = (f32[2048]{0:T(1024)}, f32[2048]{0:T(1024)S(1)}, u32[]{:S(2)}) copy-start(f32[2048]{0:T(1024)S(1)} %get-tuple-element.201) | copy-start | bytes 24580
  9.0 73.2 %copy-start.29 = (f32[2048]{0:T(1024)}, f32[2048]{0:T(1024)S(1)}, u32[]{:S(2)}) copy-start(f32[2048]{0:T(1024)S(1)} %get-tuple-element.202) | copy-start | bytes 24580
  9.0 73.2 %copy-start.31 = (f32[2048]{0:T(1024)}, f32[2048]{0:T(1024)S(1)}, u32[]{:S(2)}) copy-start(f32[2048]{0:T(1024)S(1)} %get-tuple-element.203) | copy-start | bytes 24580
  9.1 73.1 %copy-start.35 = (f32[2048]{0:T(1024)}, f32[2048]{0:T(1024)S(1)}, u32[]{:S(2)}) copy-start(f32[2048]{0:T(1024)S(1)} %get-tuple-element.205) | copy-start | bytes 24580
  9.2 73.3 %copy-start.23 = (f32[2048]{0:T(1024)}, f32[2048]{0:T(1024)S(1)}, u32[]{:S(2)}) copy-start(f32[2048]{0:T(1024)S(1)} %get-tuple-element.206) | copy-start | bytes 24580
  22.0 16.2 %all-to-all-start = ((f32[16,8,128]{2,1,0:T(8,128)}), f32[16,8,128]{2,1,0:T(8,128)S(1)}, u32[]{:S(2)}, u32[]{:S(2)}) async-start(f32[16,8,128]{2,1,0:T(8,128)} %constant_dynamic-update-slice_fusion), calls=%async_computation | async-start | bytes 131072 | tf_op jit(solution)/shard_map/all_to_all | solution.py:112
  71.1 11.0 %all-to-all-start.1 = ((f32[16,8,128]{2,1,0:T(8,128)}), f32[16,8,128]{2,1,0:T(8,128)S(1)}, u32[]{:S(2)}, u32[]{:S(2)}) async-start(f32[16,8,128]{2,1,0:T(8,128)} %fusion.342), calls=%async_computation.1 | async-start | bytes 131072 | tf_op jit(solution)/shard_map/all_to_all | solution.py:119
  83.7 18.0 %collective-permute-start = (bf16[1,1,2048]{2,1,0:T(2,128)(2,1)S(1)}, bf16[1,1,2048]{2,1,0:T(2,128)(2,1)S(1)}, u32[]{:S(2)}, u32[]{:S(2)}) collective-permute-start(bf16[1,1,2048]{2,1,0:T(2,128)(2,1)S(1)} %get-tuple-element.167), channel_id=1, source_target_pairs={{0,1},{1,2},{2,3},{3,4},{4,5},{5,6},{6,7},{7,8},{8,9},{9,10},{10,1... | collective-permute-start | bytes 12296 | tf_op jit(solution)/shard_map/ppermute | solution.py:20
  85.1 16.5 %collective-permute-start.1 = (bf16[1,1,2048]{2,1,0:T(2,128)(2,1)S(1)}, bf16[1,1,2048]{2,1,0:T(2,128)(2,1)S(1)}, u32[]{:S(2)}, u32[]{:S(2)}) collective-permute-start(bf16[1,1,2048]{2,1,0:T(2,128)(2,1)S(1)} %get-tuple-element.168), channel_id=1, source_target_pairs={{1,0},{2,1},{3,2},{4,3},{5,4},{6,5},{7,6},{8,7},{9,8},{10,9},{11,1... | collective-permute-start | bytes 12296 | tf_op jit(solution)/shard_map/ppermute | solution.py:21
  126.2 5.2 %collective-permute-start.2 = (bf16[32,1,2048]{2,0,1:T(8,128)(2,1)S(1)}, bf16[32,1,2048]{2,0,1:T(8,128)(2,1)S(1)}, u32[]{:S(2)}, u32[]{:S(2)}) collective-permute-start(bf16[32,1,2048]{2,0,1:T(8,128)(2,1)S(1)} %get-tuple-element.57), channel_id=1, source_target_pairs={{0,1},{1,2},{2,3},{3,4},{4,5},{5,6},{6,7},{7,8},{8,9},{9,10},{10,1... | collective-permute-start | bytes 393224 | tf_op jit(solution)/shard_map/ppermute | solution.py:20
  129.4 4.5 collective-permute-start.3
  204.9 18.9 %collective-permute-start.4 = (bf16[32,1,2048]{2,0,1:T(8,128)(2,1)}, bf16[32,1,2048]{2,0,1:T(8,128)(2,1)}, u32[]{:S(2)}, u32[]{:S(2)}) collective-permute-start(bf16[32,1,2048]{2,0,1:T(8,128)(2,1)} %get-tuple-element.55), channel_id=1, source_target_pairs={{0,1},{1,2},{2,3},{3,4},{4,5},{5,6},{6,7},{7,8},{8,9},{9,10},{10,1... | collective-permute-start | bytes 393224 | tf_op jit(solution)/shard_map/ppermute | solution.py:20
  211.0 12.8 %collective-permute-start.5 = (bf16[32,1,2048]{2,0,1:T(8,128)(2,1)}, bf16[32,1,2048]{2,0,1:T(8,128)(2,1)}, u32[]{:S(2)}, u32[]{:S(2)}) collective-permute-start(bf16[32,1,2048]{2,0,1:T(8,128)(2,1)} %get-tuple-element.56), channel_id=1, source_target_pairs={{1,0},{2,1},{3,2},{4,3},{5,4},{6,5},{7,6},{8,7},{9,8},{10,9},{11,1... | collective-permute-start | bytes 393224 | tf_op jit(solution)/shard_map/ppermute | solution.py:21
  212.3 7.0 %collective-permute-start.8 = (bf16[32,1,2048]{2,0,1:T(8,128)(2,1)}, bf16[32,1,2048]{2,0,1:T(8,128)(2,1)S(1)}, u32[]{:S(2)}, u32[]{:S(2)}) collective-permute-start(bf16[32,1,2048]{2,0,1:T(8,128)(2,1)} %get-tuple-element.53), channel_id=1, source_target_pairs={{0,1},{1,2},{2,3},{3,4},{4,5},{5,6},{6,7},{7,8},{8,9},{9,10},{10,1... | collective-permute-start | bytes 393224 | tf_op jit(solution)/shard_map/ppermute | solution.py:20
  215.4 5.0 %collective-permute-start.9 = (bf16[32,1,2048]{2,0,1:T(8,128)(2,1)S(1)}, bf16[32,1,2048]{2,0,1:T(8,128)(2,1)S(1)}, u32[]{:S(2)}, u32[]{:S(2)}) collective-permute-start(bf16[32,1,2048]{2,0,1:T(8,128)(2,1)S(1)} %get-tuple-element.54), channel_id=1, source_target_pairs={{1,0},{2,1},{3,2},{4,3},{5,4},{6,5},{7,6},{8,7},{9,8},{10,9},{11,1... | collective-permute-start | bytes 393224 | tf_op jit(solution)/shard_map/ppermute | solution.py:21
  306.7 7.9 %collective-permute-start.10 = (bf16[32,1,2048]{2,0,1:T(8,128)(2,1)S(1)}, bf16[32,1,2048]{2,0,1:T(8,128)(2,1)S(1)}, u32[]{:S(2)}, u32[]{:S(2)}) collective-permute-start(bf16[32,1,2048]{2,0,1:T(8,128)(2,1)S(1)} %get-tuple-element.51), channel_id=1, source_target_pairs={{0,1},{1,2},{2,3},{3,4},{4,5},{5,6},{6,7},{7,8},{8,9},{9,10},{10,1... | collective-permute-start | bytes 393224 | tf_op jit(solution)/shard_map/ppermute | solution.py:20
  312.2 3.2 collective-permute-start.11
  357.1 15.7 %all-to-all-start.2 = ((f32[16,8,128]{2,1,0:T(8,128)}), f32[16,8,128]{2,1,0:T(8,128)S(1)}, u32[]{:S(2)}, u32[]{:S(2)}) async-start(f32[16,8,128]{2,1,0:T(8,128)} %constant_dynamic-update-slice_fusion.16), calls=%async_computation.2 | async-start | bytes 131072 | tf_op jit(solution)/shard_map/all_to_all | solution.py:112
  404.9 67.7 %all-to-all-start.3 = ((f32[16,8,128]{2,1,0:T(8,128)}), f32[16,8,128]{2,1,0:T(8,128)S(1)}, u32[]{:S(2)}, u32[]{:S(2)}) async-start(f32[16,8,128]{2,1,0:T(8,128)} %fusion.341), calls=%async_computation.3 | async-start | bytes 131072 | tf_op jit(solution)/shard_map/all_to_all | solution.py:119
  (68 other events, 978.1 us)
